TPU v7x, 512 devices: a whole 4x8x8 slice. The times are simulated.
512 devices in a mesh: rows: 64 (over z, y_hi, core), chan: 8 (over y_lo, x).
Axes of the slice: x: 4, y: 8 (y_hi: 4, y_lo: 2; y = y_hi * 2 + y_lo), z: 8, core: 2. Of those that a mesh axis runs over, the one named last changes fastest.
Arguments:
- pair: bfloat16 [512, 512, 128], P('rows', 'chan'), may hold values from -6 to 6
- block_mask: int32 [4, 4], replicated, may hold values from 0 to 1, as said below
- w_in: bfloat16 [128, 640], replicated, may hold values from -0.5 to 0.5
- w_out: bfloat16 [128, 128], replicated, may hold values from -0.5 to 0.5
Outputs:
- update: bfloat16 [512, 512, 128], P('rows', 'chan')
Inputs may be any that keep to these rules, and one draw needn't show every extreme that they name: Every diagonal entry of block_mask is 1; other entries are 0 or 1.
All inputs are finite; a program needn't handle non-finite values.
Results may differ from a plain program's by a relative error of at most 0.0078.
Values may be sent and summed in bfloat16 or wider, within the bound.
A program may use at most 64 MiB of HBM per device.

v0:
```python
import jax
import jax.numpy as jnp
from jax import lax
from jax.sharding import PartitionSpec as P

BLOCK = 128


def layer_norm(values):
    mean = jnp.mean(values, axis=-1, keepdims=True)
    centered = values - mean
    var = jnp.mean(centered * centered, axis=-1, keepdims=True)
    return centered / jnp.sqrt(var + 1e-05)


def channel_product(left, piece):
    return jnp.einsum("cik,cjk->cij", left, piece, preferred_element_type=jnp.float32)


def on_device(pair, block_mask, w_in, w_out):
    rows_dev, cols_dev, width = pair.shape
    n_blocks = block_mask.shape[0]
    row_start = lax.axis_index("rows") * rows_dev
    col_start = lax.axis_index("chan") * cols_dev
    row_ids = row_start + lax.broadcasted_iota(jnp.int32, (rows_dev, n_blocks), 0)
    col_ids = col_start + lax.broadcasted_iota(jnp.int32, (cols_dev, n_blocks), 0)
    rows_hot = (
        row_ids // BLOCK == lax.broadcasted_iota(jnp.int32, (rows_dev, n_blocks), 1)
    ).astype(jnp.float32)
    cols_hot = (
        col_ids // BLOCK == lax.broadcasted_iota(jnp.int32, (cols_dev, n_blocks), 1)
    ).astype(jnp.float32)
    mask_float = block_mask.astype(jnp.float32)
    local_mask = jnp.dot(jnp.dot(rows_hot, mask_float), cols_hot.T)[:, :, None]
    normed = layer_norm(pair.astype(jnp.float32)).astype(jnp.bfloat16)
    proj = jnp.dot(normed.reshape(-1, width), w_in, preferred_element_type=jnp.float32).reshape(
        rows_dev, cols_dev, 5 * width
    )
    left = (jax.nn.sigmoid(proj[..., :width]) * proj[..., width : 2 * width] * local_mask).astype(
        jnp.bfloat16
    )
    right = (
        jax.nn.sigmoid(proj[..., 2 * width : 3 * width])
        * proj[..., 3 * width : 4 * width]
        * local_mask
    ).astype(jnp.bfloat16)
    gate = jax.nn.sigmoid(proj[..., 4 * width :])
    left_t = jnp.transpose(left, (2, 0, 1))
    right_t = jnp.transpose(right, (2, 0, 1))
    left_ch, right_ch = (
        lax.all_to_all(left_t, "chan", split_axis=0, concat_axis=2, tiled=True),
        lax.all_to_all(right_t, "chan", split_axis=0, concat_axis=2, tiled=True),
    )
    prod_ch = channel_product(left_ch, lax.all_gather(right_ch, "rows", axis=1, tiled=True))
    prod_back = lax.all_to_all(prod_ch, "chan", split_axis=2, concat_axis=0, tiled=True)
    prod = jnp.transpose(prod_back, (1, 2, 0))
    normed_prod = layer_norm(prod).astype(jnp.bfloat16)
    mixed = jnp.dot(
        normed_prod.reshape(-1, width), w_out, preferred_element_type=jnp.float32
    ).reshape(rows_dev, cols_dev, width)
    return (gate * mixed).astype(jnp.bfloat16)


def solution(mesh):
    placed = (P("rows", "chan", None), P(), P(), P())
    return jax.shard_map(
        on_device, mesh=mesh, in_specs=placed, out_specs=P("rows", "chan", None), check_vma=False
    )
```

profile of v0, /device:TPU:16, one launch (start us, length us, event | category | flops | bytes accessed | tf_op | source)
XLA Modules:
  0.0 163.1 jit_solution(1687024607968159567)
XLA Ops:
  6.5 0.0 copy-start
  6.5 0.0 all-gather.2.cloned.1.call-start
  6.6 1.1 convert_reduce_fusion
  7.7 1.2 fusion.6
  8.9 0.0 copy-done
  8.9 1.3 fusion.22
  10.2 0.0 copy-start.1
  10.2 1.1 fusion.1
  11.3 0.2 fusion.28
  11.5 0.2 copy.23
  11.7 0.2 reshape.37
  11.9 11.7 %all_to_all.54 = bf16[8,2,4096]{2,1,0:T(2,128)(2,1)S(1)} all-to-all(bf16[8,2,4096]{2,1,0:T(2,128)(2,1)S(1)} %reshape.37), channel_id=1, replica_groups=mesh['rows'=64,'chan'=8] {'chan'}, dimensions={0} | all-to-all | bytes 262144 | tf_op jit(solution)/shard_map/all_to_all | solution.py:52
  23.6 0.2 reshape.38
  23.8 0.2 copy.24
  24.0 0.9 all_to_all.46
  24.9 0.0 all-gather.2.cloned.1.call-update
  24.9 0.0 copy-done.1
  24.9 0.2 copy.21
  25.1 0.2 reshape.35
  25.4 9.1 %all_to_all.55 = bf16[8,2,4096]{2,1,0:T(2,128)(2,1)S(1)} all-to-all(bf16[8,2,4096]{2,1,0:T(2,128)(2,1)S(1)} %reshape.35), channel_id=1, replica_groups=mesh['rows'=64,'chan'=8] {'chan'}, dimensions={0} | all-to-all | bytes 262144 | tf_op jit(solution)/shard_map/all_to_all | solution.py:51
  34.5 0.2 reshape.36
  34.7 0.2 copy.22
  34.9 0.2 all_to_all.42
  35.1 93.4 %all-gather.2.cloned.1.call-done = bf16[16,512,512]{2,1,0:T(8,128)(2,1)} async-done(((bf16[16,8,512]{2,1,0:T(8,128)(2,1)}), bf16[16,512,512]{2,1,0:T(8,128)(2,1)}) %all-gather.2.cloned.1.call-update) | async-done | bytes 8388624 | tf_op jit(solution)/shard_map/all_gather | solution.py:54
  128.4 5.6 %fusion.41 = f32[16,8,512]{2,1,0:T(8,128)S(1)} fusion(bf16[16,8,512]{2,1,0:T(8,128)(2,1)S(1)} %all_to_all.42, bf16[16,512,512]{2,1,0:T(8,128)(2,1)} %all-gather.2.cloned.1.call-done), kind=kOutput, calls=%fused_computation.65 | convolution fusion | flops 67108864 | bytes 8781824 | tf_op jit(solution)/shard_map/cik,cjk->cij/dot_general | solution.py:17
  134.1 0.8 copy.25
  134.9 0.7 reshape.39
  135.7 15.2 %all_to_all.56 = f32[8,1,8192]{2,1,0:T(1,128)S(1)} all-to-all(f32[8,1,8192]{2,1,0:T(1,128)S(1)} %reshape.39), channel_id=1, replica_groups=mesh['rows'=64,'chan'=8] {'chan'}, dimensions={0} | all-to-all | bytes 524288 | tf_op jit(solution)/shard_map/all_to_all | solution.py:55
  150.9 0.5 broadcast.132
  151.4 1.3 reduce
  152.7 0.7 reshape.40
  153.4 0.0 copy-start.2
  153.4 0.6 copy.26
  154.1 0.1 bitcast_reduce_fusion
  154.2 0.1 multiply_reduce_fusion
  154.4 0.1 divide_convert_fusion
  154.4 0.0 copy-done.2
  154.4 1.8 %fusion = bf16[8,64,128]{2,1,0:T(8,128)(2,1)} fusion(f32[8,64,640]{2,1,0:T(8,128)} %copy-done.1, bf16[8,64,128]{1,0,2:T(8,128)(2,1)S(1)} %divide_convert_fusion, bf16[128,128]{1,0:T(8,128)(2,1)S(1)} %copy-done.2), kind=kOutput, calls=%fused_computation.1 | convolution fusion | flops 17104896 | bytes 557056 | tf_op jit(solution)/shard_map/dot_general | solution.py:58
  (8 shorter events, 0.1 us)
Async XLA Ops:
  6.5 2.4 %copy-start = (bf16[128,640]{1,0:T(8,128)(2,1)S(1)}, bf16[128,640]{1,0:T(8,128)(2,1)}, u32[]{:S(2)}) copy-start(bf16[128,640]{1,0:T(8,128)(2,1)} %param.6) | copy-start | bytes 491524
  6.5 121.9 %all-gather.2.cloned.1.call-start = ((), (), s32[]{:S(2)}) async-start(), calls=%async_computation.3 | async-start | bytes 8519680 | tf_op jit(solution)/shard_map/all_gather | solution.py:54
  10.2 14.7 %copy-start.1 = (f32[8,64,640]{2,1,0:T(8,128)}, f32[8,64,640]{2,1,0:T(8,128)S(1)}, u32[]{:S(2)}) copy-start(f32[8,64,640]{2,1,0:T(8,128)S(1)} %fusion.22) | copy-start | bytes 3932164
  153.4 1.0 copy-start.2
Sparse Core Ops, SparseCore 0:
  25.0 103.3 all-gather.1
where the time goes:
time: 163 us
  waiting for transfers between devices  93.4 us (57%)
  blocking collectives  36 us (22%)
  between operations  13.6 us (8%)
  matrix products  9.88 us (6%)
  local copies, waits for them, and re-layouts  6.17 us (4%)
  other arithmetic  4.1 us (3%)
    all_gather x1, waiting for transfers between devices, on_device(): lax.all_gather(right_ch, 'rows', axis=1, tiled=True)  93.4 us
    all_to_all x1, blocking collectives, on_device(): lax.all_to_all(prod_ch, 'chan', split_axis=2, concat_axis=0, tiled=True)  15.2 us
    all_to_all x1, blocking collectives, on_device(): lax.all_to_all(right_t, 'chan', split_axis=0, concat_axis=2, tiled=True)  11.7 us
    all_to_all x1, blocking collectives, on_device(): lax.all_to_all(left_t, 'chan', split_axis=0, concat_axis=2, tiled=True)  9.11 us
    dot_general x1, matrix products, channel_product(): jnp.einsum('cik,cjk->cij', left, piece, preferred_element_type=jnp.float32)  5.63 us
  transfers between devices with their start and end apart: 1, of which 1 were waited for; matrix products, arithmetic and copies ran while one was open for 0% of the time, Pallas kernels for 0%

commit v1 on v0

--- a/solution.py
+++ b/solution.py
@@ -51,7 +51,17 @@
         lax.all_to_all(left_t, "chan", split_axis=0, concat_axis=2, tiled=True),
         lax.all_to_all(right_t, "chan", split_axis=0, concat_axis=2, tiled=True),
     )
-    prod_ch = channel_product(left_ch, lax.all_gather(right_ch, "rows", axis=1, tiled=True))
+
+    def compute_the_loops(field):
+        fresh = jax.lax.all_to_all(
+            jnp.stack(jax.lax.axis_size("rows") * [field]),
+            axis_name="rows",
+            split_axis=0,
+            concat_axis=0,
+        )
+        return jnp.concatenate(fresh, axis=1)
+
+    prod_ch = channel_product(left_ch, compute_the_loops(right_ch))
     prod_back = lax.all_to_all(prod_ch, "chan", split_axis=2, concat_axis=0, tiled=True)
     prod = jnp.transpose(prod_back, (1, 2, 0))
     normed_prod = layer_norm(prod).astype(jnp.bfloat16)

time: 163 us -> 301 us (1.85)
  the two profiles are of different devices: /device:TPU:16 before, /device:TPU:144 now
where the time goes in v1:
time: 301 us; the launch traced here: 300 us
  waiting for transfers between devices  221 us (73%)
  blocking collectives  31.2 us (10%)
  starting transfers between devices  22.6 us (8%)
  local copies, waits for them, and re-layouts  11 us (4%)
  matrix products  9.89 us (3%)
  other arithmetic  4.1 us (1%)
    all_to_all x1, waiting for transfers between devices, compute_the_loops(): jax.lax.all_to_all(jnp.stack(jax.lax.axis_size('rows') * [field]), axis_n...  210 us
    all_to_all x1, blocking collectives, on_device(): lax.all_to_all(prod_ch, 'chan', split_axis=2, concat_axis=0, tiled=True)  31.2 us
    all_to_all x1, starting transfers between devices, compute_the_loops(): jax.lax.all_to_all(jnp.stack(jax.lax.axis_size('rows') * [field]), axis_n...  13.9 us
  transfers between devices with their start and end apart: 3, of which 3 were waited for; matrix products, arithmetic and copies ran while one was open for 1% of the time, Pallas kernels for 0%

profile of v1, /device:TPU:144, one launch (start us, length us, event | category | flops | bytes accessed | tf_op | source)
XLA Modules:
  0.0 300.2 jit_solution(16976261848968433075)
XLA Ops:
  0.0 0.0 copy-start
  0.1 1.1 convert_reduce_fusion
  1.2 1.2 fusion.9
  2.3 0.0 copy-done
  2.4 1.3 fusion.25
  3.7 0.0 copy-start.1
  3.7 1.1 fusion.4
  4.8 0.2 fusion.31
  5.0 0.2 copy.23
  5.1 0.9 reshape.48
  6.0 5.3 %all-to-all-start.1 = ((bf16[8,2,4096]{2,1,0:T(2,128)(2,1)}), bf16[8,2,4096]{2,1,0:T(2,128)(2,1)S(1)}, u32[]{:S(2)}, u32[]{:S(2)}) async-start(bf16[8,2,4096]{2,1,0:T(2,128)(2,1)} %reshape.48), calls=%async_computation.1 | async-start | bytes 262144 | tf_op jit(solution)/shard_map/all_to_all | solution.py:52
  11.3 0.2 copy.21
  11.5 0.9 reshape.46
  12.4 5.5 %all-to-all-done.1 = bf16[8,2,4096]{2,1,0:T(2,128)(2,1)S(1)} async-done(((bf16[8,2,4096]{2,1,0:T(2,128)(2,1)}), bf16[8,2,4096]{2,1,0:T(2,128)(2,1)S(1)}, u32[]{:S(2)}, u32[]{:S(2)}) %all-to-all-start.1) | async-done | bytes 131104 | tf_op jit(solution)/shard_map/all_to_all | solution.py:52
  17.9 3.4 %all-to-all-start = ((bf16[8,2,4096]{2,1,0:T(2,128)(2,1)}), bf16[8,2,4096]{2,1,0:T(2,128)(2,1)S(1)}, u32[]{:S(2)}, u32[]{:S(2)}) async-start(bf16[8,2,4096]{2,1,0:T(2,128)(2,1)} %reshape.46), calls=%async_computation | async-start | bytes 262144 | tf_op jit(solution)/shard_map/all_to_all | solution.py:51
  21.3 0.2 reshape.49
  21.5 0.2 copy.24
  21.7 0.2 stack.4
  21.9 5.9 %all-to-all-done = bf16[8,2,4096]{2,1,0:T(2,128)(2,1)S(1)} async-done(((bf16[8,2,4096]{2,1,0:T(2,128)(2,1)}), bf16[8,2,4096]{2,1,0:T(2,128)(2,1)S(1)}, u32[]{:S(2)}, u32[]{:S(2)}) %all-to-all-start) | async-done | bytes 131104 | tf_op jit(solution)/shard_map/all_to_all | solution.py:51
  27.8 4.2 %stack.5 = bf16[64,16,8,512]{3,2,1,0:T(8,128)(2,1)} broadcast(bf16[16,8,512]{2,1,0:T(8,128)(2,1)S(1)} %stack.4), dimensions={1,2,3} | broadcast | bytes 8519680 | tf_op jit(solution)/shard_map/stack | solution.py:57
  32.0 0.0 copy-done.1
  32.0 13.9 %all-to-all-start.2 = ((bf16[64,16,8,512]{3,2,1,0:T(8,128)(2,1)}), bf16[64,16,8,512]{3,2,1,0:T(8,128)(2,1)}, u32[]{:S(2)}, u32[]{:S(2)}) async-start(bf16[64,16,8,512]{3,2,1,0:T(8,128)(2,1)} %stack.5), calls=%async_computation.2 | async-start | bytes 16777216 | tf_op jit(solution)/shard_map/all_to_all | solution.py:56
  46.0 0.2 reshape.47
  46.2 0.2 copy.22
  46.4 0.2 all_to_all.43
  46.6 209.7 %all-to-all-done.2 = bf16[64,16,8,512]{3,2,1,0:T(8,128)(2,1)} async-done(((bf16[64,16,8,512]{3,2,1,0:T(8,128)(2,1)}), bf16[64,16,8,512]{3,2,1,0:T(8,128)(2,1)}, u32[]{:S(2)}, u32[]{:S(2)}) %all-to-all-start.2) | async-done | bytes 8388640 | tf_op jit(solution)/shard_map/all_to_all | solution.py:56
  256.3 5.6 %fusion = f32[16,8,512]{2,1,0:T(8,128)S(1)} fusion(bf16[16,8,512]{2,1,0:T(8,128)(2,1)S(1)} %all_to_all.43, bf16[64,16,8,512]{3,2,1,0:T(8,128)(2,1)} %all-to-all-done.2), kind=kOutput, calls=%fused_computation | convolution fusion | flops 67108864 | bytes 8781824 | tf_op jit(solution)/shard_map/cik,cjk->cij/dot_general | solution.py:17
  262.0 0.0 copy-start.2
  262.0 0.8 copy.26
  262.8 0.7 reshape.50
  263.6 31.2 %all_to_all.56 = f32[8,1,8192]{2,1,0:T(1,128)S(1)} all-to-all(f32[8,1,8192]{2,1,0:T(1,128)S(1)} %reshape.50), channel_id=1, replica_groups=mesh['rows'=64,'chan'=8] {'chan'}, dimensions={0} | all-to-all | bytes 524288 | tf_op jit(solution)/shard_map/all_to_all | solution.py:65
  294.8 0.5 broadcast.133
  295.3 1.3 reduce
  296.6 0.7 reshape.51
  297.3 0.6 copy.27
  297.9 0.1 bitcast_reduce_fusion
  298.1 0.1 multiply_reduce_fusion
  298.2 0.1 divide_convert_fusion
  298.3 0.0 copy-done.2
  298.3 1.8 fusion.3
  (8 shorter events, 0.1 us)
Async XLA Ops:
  0.0 2.3 copy-start
  3.7 28.4 %copy-start.1 = (f32[8,64,640]{2,1,0:T(8,128)}, f32[8,64,640]{2,1,0:T(8,128)S(1)}, u32[]{:S(2)}) copy-start(f32[8,64,640]{2,1,0:T(8,128)S(1)} %fusion.25) | copy-start | bytes 3932164
  6.0 11.9 %all-to-all-start.1 = ((bf16[8,2,4096]{2,1,0:T(2,128)(2,1)}), bf16[8,2,4096]{2,1,0:T(2,128)(2,1)S(1)}, u32[]{:S(2)}, u32[]{:S(2)}) async-start(bf16[8,2,4096]{2,1,0:T(2,128)(2,1)} %reshape.48), calls=%async_computation.1 | async-start | bytes 262144 | tf_op jit(solution)/shard_map/all_to_all | solution.py:52
  17.9 9.9 %all-to-all-start = ((bf16[8,2,4096]{2,1,0:T(2,128)(2,1)}), bf16[8,2,4096]{2,1,0:T(2,128)(2,1)S(1)}, u32[]{:S(2)}, u32[]{:S(2)}) async-start(bf16[8,2,4096]{2,1,0:T(2,128)(2,1)} %reshape.46), calls=%async_computation | async-start | bytes 262144 | tf_op jit(solution)/shard_map/all_to_all | solution.py:51
  32.0 224.3 %all-to-all-start.2 = ((bf16[64,16,8,512]{3,2,1,0:T(8,128)(2,1)}), bf16[64,16,8,512]{3,2,1,0:T(8,128)(2,1)}, u32[]{:S(2)}, u32[]{:S(2)}) async-start(bf16[64,16,8,512]{3,2,1,0:T(8,128)(2,1)} %stack.5), calls=%async_computation.2 | async-start | bytes 16777216 | tf_op jit(solution)/shard_map/all_to_all | solution.py:56
  262.0 36.3 %copy-start.2 = (bf16[128,128]{1,0:T(8,128)(2,1)S(1)}, bf16[128,128]{1,0:T(8,128)(2,1)}, u32[]{:S(2)}) copy-start(bf16[128,128]{1,0:T(8,128)(2,1)} %param.7) | copy-start | bytes 98308
